TPU v7x, 128 devices: a whole 4x4x4 slice. The times are simulated.
128 devices in a mesh: row: 8 (over x, core), col: 16 (over y, z).
Axes of the slice: x: 4, y: 4, z: 4, core: 2. Of those that a mesh axis runs over, the one named last changes fastest.
Arguments:
- parent_front: float32 [16384, 16384], P('row', 'col'), as said below
- child_panels: float32 [8, 4096, 512], P('row', 'col'), may hold values from -6 to 6
- child_inverses: float32 [8, 512, 512], P('row'), as said below
- parent_index: int32 [8, 16], replicated, may hold values from 2 to 63, as said below
Outputs:
- panel: float32 [16384, 512], P('row')
- schur: float32 [16384, 16384], P('row', 'col')
Inputs may be any that keep to these rules, and one draw needn't show every extreme that they name: `parent_index`: entry (g, u) names the parent tile that receives tile row and tile column u of child g's update. Seen in blocks of 4 consecutive tiles, each child names every block exactly once, and at a given u the children name different blocks. No entry names one of the first 2 tiles. `parent_front`: Symmetric. In its leading 2 * 256 rows and columns, each diagonal entry is positive and exceeds the sum of magnitudes of the other entries of its row within that block. `child_inverses`: each matrix is lower triangular with a positive diagonal.
All inputs are finite; a program needn't handle non-finite values.
Results may differ from a plain program's by a relative error of at most 0.0003.
Values sent between devices are 32-bit elements; how exact they have to be, the bound alone decides.
A program may use at most 128 MiB of HBM per device.

v0:
```python
import jax
import jax.numpy as jnp
from jax import lax
from jax.sharding import PartitionSpec as P

TILE = 256
PCT = 4
NSP = 2


def from_root(block, axis, holder):
    block = jnp.where(lax.axis_index(axis) == holder, block, jnp.zeros_like(block))
    return lax.psum(block, axis)


def product(matrix_a, matrix_b):
    return jnp.dot(
        matrix_a, matrix_b, precision=lax.Precision.HIGHEST, preferred_element_type=jnp.float32
    )


def product_rows(matrix_a, matrix_b):
    return lax.dot_general(
        matrix_a,
        matrix_b,
        (((1,), (1,)), ((), ())),
        precision=lax.Precision.HIGHEST,
        preferred_element_type=jnp.float32,
    )


def place_tiles(received, row_tiles, col_tiles, live_mask, tile_count):
    target = row_tiles * PCT + col_tiles
    onehot = (target[None, :] == jnp.arange(tile_count)[:, None]).astype(jnp.float32) * live_mask[
        None, :
    ]
    flat_tiles = received.reshape(received.shape[0], TILE * TILE)
    return product(onehot, flat_tiles)


def per_device(parent_front, child_panels, child_inverses, parent_index):
    row_devices = lax.axis_size("row")
    col_devices = lax.axis_size("col")
    here_row = lax.axis_index("row")
    here_col = lax.axis_index("col")
    per_block = col_devices // row_devices
    row_count = PCT * per_block
    tile_count = row_count * PCT
    own_factor = product_rows(child_panels[0], child_inverses[0])
    my_list = lax.dynamic_index_in_dim(parent_index, here_row, 0, keepdims=False)
    block_of = parent_index // PCT
    update_col = product_rows(lax.all_gather(own_factor, "col", axis=0, tiled=True), own_factor)
    dest_row = my_list // PCT // per_block
    tile_ids = jnp.arange(col_devices, dtype=jnp.int32)
    same_dest = (dest_row[None, :] == dest_row[:, None]) & (tile_ids[None, :] < tile_ids[:, None])
    slot_index = jnp.sum(same_dest.astype(jnp.int32), axis=1)
    position = dest_row * per_block + slot_index
    send_order = jnp.zeros((col_devices,), jnp.int32).at[position].set(tile_ids)
    outgoing = update_col.reshape(col_devices, TILE, TILE)[send_order].reshape(
        row_devices, per_block, TILE, TILE
    )
    arrived = lax.all_to_all(outgoing, "row", split_axis=0, concat_axis=0, tiled=True)
    local_mask = block_of // per_block == here_row
    slot_rank = jnp.cumsum(local_mask.astype(jnp.int32), axis=1) - 1
    slot_ids = jnp.arange(per_block, dtype=jnp.int32)
    slot_pick = (
        local_mask[:, :, None] & (slot_rank[:, :, None] == slot_ids[None, None, :])
    ).astype(jnp.int32)
    row_tile = jnp.sum(parent_index[:, :, None] * slot_pick, axis=1) - here_row * row_count
    sent_to = lax.dynamic_index_in_dim(block_of, here_col, 1, keepdims=False)
    col_route = (sent_to[None, :] == jnp.arange(col_devices)[:, None]).astype(jnp.float32)
    outgoing_cols = product(col_route, arrived.reshape(row_devices, -1)).reshape(
        col_devices, per_block, TILE, TILE
    )
    arrived_cols = lax.all_to_all(outgoing_cols, "col", split_axis=0, concat_axis=0, tiled=True)
    col_match = (block_of == here_col).astype(jnp.int32)
    col_tile = parent_index - here_col * PCT
    rows_from = jnp.sum(row_tile[:, None, :] * col_match[:, :, None], axis=0)
    cols_from = jnp.sum(col_tile * col_match, axis=0)
    live_from = jnp.sum(col_match, axis=0).astype(jnp.float32)
    cols_flat = (cols_from[:, None] + jnp.zeros_like(rows_from)).reshape(-1)
    live_flat = (live_from[:, None] + jnp.zeros(rows_from.shape, jnp.float32)).reshape(-1)
    contrib = place_tiles(
        arrived_cols.reshape(-1, TILE, TILE),
        rows_from.reshape(-1),
        cols_flat,
        live_flat,
        tile_count,
    )
    contrib = (
        contrib.reshape(row_count, PCT, TILE, TILE)
        .transpose(0, 2, 1, 3)
        .reshape(row_count * TILE, PCT * TILE)
    )
    work_matrix = parent_front - contrib
    identity = jnp.eye(TILE, dtype=jnp.float32)
    owner = (here_row == 0) & (here_col == 0)
    row_tile_index = here_row * row_count + jnp.arange(row_count * TILE) // TILE
    columns = []
    for step in range(NSP):
        offset = step * TILE
        diag_tile = jnp.where(
            owner, work_matrix[offset : offset + TILE, offset : offset + TILE], identity
        )
        pivot_tile = jnp.linalg.cholesky(diag_tile)
        inverse = lax.linalg.triangular_solve(pivot_tile, identity, left_side=True, lower=True)
        pivot_pair = from_root(jnp.stack([pivot_tile, inverse]), "row", 0)
        pivot_tile = pivot_pair[0]
        inverse = pivot_pair[1]
        factored = product_rows(work_matrix[:, offset : offset + TILE], inverse)
        factored = jnp.where(row_tile_index[:, None] < step, jnp.zeros_like(factored), factored)
        current = factored[offset : offset + TILE]
        rows_panel, inverse = (
            from_root(
                factored.at[offset : offset + TILE].set(
                    jnp.where(here_row == 0, pivot_tile, current)
                ),
                "col",
                0,
            ),
            from_root(inverse, "col", 0),
        )
        source = from_root(rows_panel, "row", here_col // per_block)
        col_panel = lax.dynamic_slice_in_dim(
            source, here_col % per_block * PCT * TILE, PCT * TILE, 0
        )
        work_matrix = work_matrix - product_rows(rows_panel, col_panel)
        columns.append(rows_panel)
    return (jnp.concatenate(columns, axis=1), work_matrix)


def solution(mesh):
    placed = (P("row", "col"), P("row", "col", None), P("row", None, None), P())
    return jax.shard_map(
        per_device,
        mesh=mesh,
        in_specs=placed,
        out_specs=(P("row", None), P("row", "col")),
        check_vma=False,
    )
```

profile of v0, /device:TPU:0, one launch (start us, length us, event | category | flops | bytes accessed | tf_op | source)
XLA Modules:
  0.0 993.7 jit_solution(9929762409883196764)
XLA Ops:
  14.3 70.5 %all-gather.2.cloned.1.call-done = f32[4096,512]{1,0:T(8,128)} async-done(((f32[256,512]{1,0:T(8,128)}), f32[4096,512]{1,0:T(8,128)}) %all-gather.2.cloned.1.call-update) | async-done | bytes 8388624 | tf_op jit(solution)/shard_map/all_gather | solution.py:52
  84.8 10.6 %fusion.69 = f32[4096,256]{1,0:T(8,128)} fusion(f32[4096,512]{1,0:T(8,128)} %all-gather.2.cloned.1.call-done, f32[256,512]{1,0:T(8,128)} %fusion.5), kind=kOutput, calls=%fused_computation.186 | convolution fusion | flops 6442450944 | bytes 13107200 | tf_op jit(solution)/shard_map/dot_general | solution.py:23
  105.5 49.4 %all-to-all-done = f32[8,2,256,256]{3,2,1,0:T(8,128)} async-done(((f32[8,2,256,256]{3,2,1,0:T(8,128)}), f32[8,2,256,256]{3,2,1,0:T(8,128)}, u32[]{:S(2)}, u32[]{:S(2)}) %all-to-all-start) | async-done | bytes 4194336 | tf_op jit(solution)/shard_map/all_to_all | solution.py:62
  186.9 134.8 %all-to-all-done.1 = f32[16,2,256,256]{3,2,1,0:T(8,128)} async-done(((f32[16,2,256,256]{3,2,1,0:T(8,128)}), f32[16,2,256,256]{3,2,1,0:T(8,128)}, u32[]{:S(2)}, u32[]{:S(2)}) %all-to-all-start.1) | async-done | bytes 8388640 | tf_op jit(solution)/shard_map/all_to_all | solution.py:75
  321.7 17.3 %fusion.2 = f32[8,256,4,256]{3,0,1,2:T(8,128)} fusion(f32[32]{0:T(128)S(1)} %mul.78, s32[8,4]{0,1:T(4,128)S(1)} %multiply_add_fusion, s32[32]{0:T(128)S(1)} %add.154, f32[4,8,256,256]{3,2,1,0:T(8,128)} %bitcast.51), kind=kOutput, calls=%fused_computation.12 | convolution fusion | flops 805308416 | bytes 16777600 | tf_op jit(solution)/shard_map/dot_general | solution.py:17
  339.0 10.8 %copy.36 = f32[8,256,4,256]{1,0,3,2:T(8,128)} copy(f32[8,256,4,256]{3,0,1,2:T(8,128)} %fusion.2) | data formatting | bytes 16777216 | tf_op jit(solution)/shard_map/transpose | solution.py:92
  349.8 10.7 %copy.54 = f32[128,8,8,256]{3,1,2,0:T(8,128)} copy(f32[128,8,8,256]{3,2,1,0:T(8,128)} %bitcast.170) | data formatting | bytes 16777216
  360.5 11.9 %sub.79 = f32[2048,1024]{0,1:T(8,128)} subtract(f32[2048,1024]{0,1:T(8,128)} %copy.37, f32[2048,1024]{0,1:T(8,128)} %bitcast.169) | non-fusion elementwise | flops 2097152 | bytes 25165824 | tf_op jit(solution)/shard_map/sub | solution.py:95
  374.5 11.7 %cholesky.130 = f32[128,128]{1,0:T(8,128)S(1)} custom-call(f32[128,128]{1,0:T(8,128)S(1)} %cholesky.194), custom_call_target="Cholesky" | custom-call | tf_op jit(solution)/shard_map/jit(cholesky)/cholesky | solution.py:105
  386.3 10.0 %custom-call.13 = f32[1,128,128]{1,2,0:T(8,128)S(1)} custom-call(f32[1,128,128]{2,1,0:T(8,128)S(1)} %get-tuple-element.90), custom_call_target="InvertDiagBlocksLowerTriangular" | custom-call | tf_op jit(solution)/shard_map/jit(cholesky)/cholesky | solution.py:105
  396.7 11.7 %cholesky.147 = f32[128,128]{1,0:T(8,128)S(1)} custom-call(f32[128,128]{1,0:T(8,128)S(1)} %convolution_subtract_fusion.5), custom_call_target="Cholesky" | custom-call | tf_op jit(solution)/shard_map/jit(cholesky)/cholesky | solution.py:105
  414.7 19.7 %custom-call.14 = f32[2,128,128]{1,2,0:T(8,128)S(1)} custom-call(f32[2,128,128]{2,1,0:T(8,128)S(1)} %get-tuple-element.42), custom_call_target="InvertDiagBlocksLowerTriangular" | custom-call | tf_op jit(solution)/shard_map/triangular_solve/custom-call.0 | solution.py:106
  436.3 63.0 %all-reduce.8.cloned.1.call-done = f32[2,256,256]{2,1,0:T(8,128)} async-done(((f32[2,256,256]{2,1,0:T(8,128)}), f32[2,256,256]{2,1,0:T(8,128)}) %all-reduce.8.cloned.1.call-update) | async-done | bytes 524304 | tf_op jit(solution)/shard_map/psum | solution.py:13
  506.1 89.7 %all-reduce.10.cloned.1.call-done = f32[2048,256]{1,0:T(8,128)} async-done(((f32[2048,256]{1,0:T(8,128)}), f32[2048,256]{1,0:T(8,128)}) %all-reduce.10.cloned.1.call-update) | async-done | bytes 2097168 | tf_op jit(solution)/shard_map/psum | solution.py:13
  599.1 64.4 %all-reduce.12.cloned.1.call-done = f32[2048,256]{1,0:T(8,128)} async-done(((f32[2048,256]{1,0:T(8,128)}), f32[2048,256]{1,0:T(8,128)}) %all-reduce.12.cloned.1.call-update) | async-done | bytes 2097168 | tf_op jit(solution)/shard_map/psum | solution.py:13
  663.6 10.5 %convolution_subtract_fusion.1 = f32[2048,1024]{0,1:T(8,128)S(1)} fusion(f32[2048,1024]{0,1:T(8,128)} %sub.79, f32[2048,256]{1,0:T(8,128)S(1)} %copy-done.3, f32[2048,256]{1,0:T(8,128)} %all-reduce.12.cloned.1.call-done, s32[]{:T(128)S(6)} %select_n.189), kind=kOutput, calls=%fused_computation.10 | convolution fusion | flops 6444548096 | bytes 19922948 | tf_op jit(solution)/shard_map/dot_general | solution.py:23
  678.6 11.7 %cholesky.164 = f32[128,128]{1,0:T(8,128)S(1)} custom-call(f32[128,128]{1,0:T(8,128)S(1)} %cholesky.197), custom_call_target="Cholesky" | custom-call | tf_op jit(solution)/shard_map/jit(cholesky)/cholesky | solution.py:105
  691.0 9.8 custom-call.15
  701.3 11.7 %cholesky.181 = f32[128,128]{1,0:T(8,128)S(1)} custom-call(f32[128,128]{1,0:T(8,128)S(1)} %convolution_subtract_fusion.4), custom_call_target="Cholesky" | custom-call | tf_op jit(solution)/shard_map/jit(cholesky)/cholesky | solution.py:105
  719.3 19.9 %custom-call.16 = f32[2,128,128]{1,2,0:T(8,128)S(1)} custom-call(f32[2,128,128]{2,1,0:T(8,128)S(1)} %get-tuple-element.43), custom_call_target="InvertDiagBlocksLowerTriangular" | custom-call | tf_op jit(solution)/shard_map/triangular_solve/custom-call.0 | solution.py:106
  741.2 60.2 %all-reduce.14.cloned.1.call-done = f32[2,256,256]{2,1,0:T(8,128)} async-done(((f32[2,256,256]{2,1,0:T(8,128)}), f32[2,256,256]{2,1,0:T(8,128)}) %all-reduce.14.cloned.1.call-update) | async-done | bytes 524304 | tf_op jit(solution)/shard_map/psum | solution.py:13
  808.2 89.8 %all-reduce.16.cloned.1.call-done = f32[2048,256]{1,0:T(8,128)} async-done(((f32[2048,256]{1,0:T(8,128)}), f32[2048,256]{1,0:T(8,128)}) %all-reduce.16.cloned.1.call-update) | async-done | bytes 2097168 | tf_op jit(solution)/shard_map/psum | solution.py:13
  905.3 60.0 %all-reduce.18.cloned.1.call-done = f32[2048,256]{1,0:T(8,128)} async-done(((f32[2048,256]{1,0:T(8,128)}), f32[2048,256]{1,0:T(8,128)}) %all-reduce.18.cloned.1.call-update) | async-done | bytes 2097168 | tf_op jit(solution)/shard_map/psum | solution.py:13
  965.3 11.8 %convolution_subtract_fusion = f32[2048,1024]{0,1:T(8,128)} fusion(f32[2048,1024]{0,1:T(8,128)} %copy-done.2, f32[2048,256]{1,0:T(8,128)} %all-reduce.16.cloned.1.call-done, f32[2048,256]{1,0:T(8,128)} %all-reduce.18.cloned.1.call-done, s32[]{:T(128)S(6)} %select_n.189), kind=kOutput, calls=%fused_computation.9 | convolution fusion | flops 6444548096 | bytes 19922948 | tf_op jit(solution)/shard_map/dot_general | solution.py:23
  (124 shorter events, 112.5 us)
Async XLA Ops:
  7.2 1.2 copy-start
  7.2 77.6 %all-gather.2.cloned.1.call-start = ((), (), s32[]{:S(2)}) async-start(), calls=%async_computation.2 | async-start | bytes 8912896 | tf_op jit(solution)/shard_map/all_gather | solution.py:52
  100.4 4.9 copy-start.6
  100.4 54.5 %all-to-all-start = ((f32[8,2,256,256]{3,2,1,0:T(8,128)}), f32[8,2,256,256]{3,2,1,0:T(8,128)}, u32[]{:S(2)}, u32[]{:S(2)}) async-start(f32[8,2,256,256]{3,2,1,0:T(8,128)} %bitcast.172), calls=%async_computation | async-start | bytes 8388608 | tf_op jit(solution)/shard_map/all_to_all | solution.py:62
  171.3 150.4 %all-to-all-start.1 = ((f32[16,2,256,256]{3,2,1,0:T(8,128)}), f32[16,2,256,256]{3,2,1,0:T(8,128)}, u32[]{:S(2)}, u32[]{:S(2)}) async-start(f32[16,2,256,256]{3,2,1,0:T(8,128)} %copy.34), calls=%async_computation.1 | async-start | bytes 16777216 | tf_op jit(solution)/shard_map/all_to_all | solution.py:75
  176.7 322.7 %all-reduce.8.cloned.1.call-start = ((), (), s32[]{:S(2)}) async-start(), calls=%async_computation.3 | async-start | bytes 1048576 | tf_op jit(solution)/shard_map/psum | solution.py:13
  436.3 159.6 %all-reduce.10.cloned.1.call-start = ((), (), s32[]{:S(2)}) async-start(), calls=%async_computation.4 | async-start | bytes 4194304 | tf_op jit(solution)/shard_map/psum | solution.py:13
  499.3 5.2 copy-start.5
  506.0 157.5 %all-reduce.12.cloned.1.call-start = ((), (), s32[]{:S(2)}) async-start(), calls=%async_computation.5 | async-start | bytes 4194304 | tf_op jit(solution)/shard_map/psum | solution.py:13
  595.8 67.7 %copy-start.3 = (f32[2048,256]{1,0:T(8,128)S(1)}, f32[2048,256]{1,0:T(8,128)}, u32[]{:S(2)}) copy-start(f32[2048,256]{1,0:T(8,128)} %all-reduce.10.cloned.1.call-done) | copy-start | bytes 6291460
  599.1 202.4 %all-reduce.14.cloned.1.call-start = ((), (), s32[]{:S(2)}) async-start(), calls=%async_computation.6 | async-start | bytes 1048576 | tf_op jit(solution)/shard_map/psum | solution.py:13
  674.0 3.4 copy-start.2
  741.2 156.8 %all-reduce.16.cloned.1.call-start = ((), (), s32[]{:S(2)}) async-start(), calls=%async_computation.7 | async-start | bytes 4194304 | tf_op jit(solution)/shard_map/psum | solution.py:13
  801.5 5.2 copy-start.4
  808.2 157.1 %all-reduce.18.cloned.1.call-start = ((), (), s32[]{:S(2)}) async-start(), calls=%async_computation.8 | async-start | bytes 4194304 | tf_op jit(solution)/shard_map/psum | solution.py:13
  977.1 9.3 copy-start.1
Sparse Core Ops, SparseCore 0:
  11.4 73.3 all-gather.1
  436.4 62.9 all-reduce.7
  506.2 89.6 all-reduce.9
  599.2 64.3 all-reduce.11
  741.3 60.1 all-reduce.13
  808.3 89.6 all-reduce.15
  901.2 64.0 all-reduce.17
where the time goes:
time: 999 us; the launch traced here: 994 us
  waiting for transfers between devices  682 us (68%)
  other arithmetic  141 us (14%)
  local copies, waits for them, and re-layouts  71.9 us (7%)
  matrix products  70 us (7%)
  between operations  17.6 us (2%)
  starting transfers between devices  10.7 us (1%)
    psum x6, waiting for transfers between devices, from_root(): return lax.psum(block, axis)  427 us
    all_to_all x1, waiting for transfers between devices, per_device(): lax.all_to_all(outgoing_cols, 'col', split_axis=0, concat_axis=0, tiled=T...  135 us
    all_gather x1, waiting for transfers between devices, per_device(): lax.all_gather(own_factor, 'col', axis=0, tiled=True)  70.5 us
    another operation x13, other arithmetic, per_device(): pivot_tile = jnp.linalg.cholesky(diag_tile)  68.8 us
    all_to_all x1, waiting for transfers between devices, per_device(): lax.all_to_all(outgoing, 'row', split_axis=0, concat_axis=0, tiled=True)  49.4 us
    dot_general x6, matrix products, product_rows(): lax.dot_general(matrix_a, matrix_b, (((1,), (1,)), ((), ())), precision=l...  46 us
    another operation x3, other arithmetic, per_device(): lax.linalg.triangular_solve(pivot_tile, identity, left_side=True, lower=T...  39.6 us
    unnamed x18, local copies, waits for them, and re-layouts  38.4 us
  transfers between devices with their start and end apart: 9, of which 9 were waited for; matrix products, arithmetic and copies ran while one was open for 2% of the time, Pallas kernels for 0%

commit v1 on v0

--- a/solution.py
+++ b/solution.py
@@ -49,7 +49,12 @@
     own_factor = product_rows(child_panels[0], child_inverses[0])
     my_list = lax.dynamic_index_in_dim(parent_index, here_row, 0, keepdims=False)
     block_of = parent_index // PCT
-    update_col = product_rows(lax.all_gather(own_factor, "col", axis=0, tiled=True), own_factor)
+    update_col = product_rows(
+        jnp.concatenate(
+            lax.all_to_all(jnp.stack([own_factor] * lax.axis_size("col")), "col", 0, 0), axis=0
+        ),
+        own_factor,
+    )
     dest_row = my_list // PCT // per_block
     tile_ids = jnp.arange(col_devices, dtype=jnp.int32)
     same_dest = (dest_row[None, :] == dest_row[:, None]) & (tile_ids[None, :] < tile_ids[:, None])

time: 999 us -> 1090 us (1.091)
  waiting for transfers between devices: 682 us -> 758 us
  starting transfers between devices: 10.7 us -> 21.9 us
    all_to_all x0 -> x1, waiting for transfers between devices: none -> 147 us  [per_device(): lax.all_to_all(jnp.stack([own_factor] * lax.axis_size('col')), 'col', 0, 0)]
    all_gather x1 -> x0, waiting for transfers between devices: 70.5 us -> none  [per_device(): lax.all_gather(own_factor, 'col', axis=0, tiled=True)]
  transfers between devices with their start and end apart: 9 -> 9, of which waited for: 9 -> 9; matrix products, arithmetic and copies ran while one was open for 2% -> 1% of each run, Pallas kernels for 0% -> 0%
where the time goes in v1:
time: 1090 us; the launch traced here: 1080 us
  waiting for transfers between devices  758 us (70%)
  other arithmetic  139 us (13%)
  local copies, waits for them, and re-layouts  76.4 us (7%)
  matrix products  69.1 us (6%)
  starting transfers between devices  21.9 us (2%)
  between operations  17.6 us (2%)
    psum x6, waiting for transfers between devices, from_root(): return lax.psum(block, axis)  427 us
    all_to_all x1, waiting for transfers between devices, per_device(): lax.all_to_all(jnp.stack([own_factor] * lax.axis_size('col')), 'col', 0, 0)  147 us
    all_to_all x1, waiting for transfers between devices, per_device(): lax.all_to_all(outgoing_cols, 'col', split_axis=0, concat_axis=0, tiled=T...  135 us
    another operation x13, other arithmetic, per_device(): pivot_tile = jnp.linalg.cholesky(diag_tile)  68.8 us
    all_to_all x1, waiting for transfers between devices, per_device(): lax.all_to_all(outgoing, 'row', split_axis=0, concat_axis=0, tiled=True)  49.4 us
    dot_general x6, matrix products, product_rows(): lax.dot_general(matrix_a, matrix_b, (((1,), (1,)), ((), ())), precision=l...  45.1 us
    another operation x3, other arithmetic, per_device(): lax.linalg.triangular_solve(pivot_tile, identity, left_side=True, lower=T...  39.6 us
    unnamed x18, local copies, waits for them, and re-layouts  38.4 us
  transfers between devices with their start and end apart: 9, of which 9 were waited for; matrix products, arithmetic and copies ran while one was open for 1% of the time, Pallas kernels for 0%

profile of v1, /device:TPU:0, one launch (start us, length us, event | category | flops | bytes accessed | tf_op | source)
XLA Modules:
  0.0 1082.7 jit_solution(16493624821512441058)
XLA Ops:
  24.2 146.7 %all-to-all-done = f32[16,256,512]{2,1,0:T(8,128)} async-done(((f32[16,256,512]{2,1,0:T(8,128)}), f32[16,256,512]{2,1,0:T(8,128)}, u32[]{:S(2)}, u32[]{:S(2)}) %all-to-all-start) | async-done | bytes 8388640 | tf_op jit(solution)/shard_map/all_to_all | solution.py:54
  171.0 10.5 fusion.9
  191.4 49.4 %all-to-all-done.1 = f32[8,2,256,256]{3,2,1,0:T(8,128)} async-done(((f32[8,2,256,256]{3,2,1,0:T(8,128)}), f32[8,2,256,256]{3,2,1,0:T(8,128)}, u32[]{:S(2)}, u32[]{:S(2)}) %all-to-all-start.1) | async-done | bytes 4194336 | tf_op jit(solution)/shard_map/all_to_all | solution.py:67
  275.9 134.8 %all-to-all-done.2 = f32[16,2,256,256]{3,2,1,0:T(8,128)} async-done(((f32[16,2,256,256]{3,2,1,0:T(8,128)}), f32[16,2,256,256]{3,2,1,0:T(8,128)}, u32[]{:S(2)}, u32[]{:S(2)}) %all-to-all-start.2) | async-done | bytes 8388640 | tf_op jit(solution)/shard_map/all_to_all | solution.py:80
  410.7 17.3 %fusion.2 = f32[8,256,4,256]{3,0,1,2:T(8,128)} fusion(f32[32]{0:T(128)S(1)} %mul.78, s32[8,4]{0,1:T(4,128)S(1)} %multiply_add_fusion, s32[32]{0:T(128)S(1)} %add.154, f32[4,8,256,256]{3,2,1,0:T(8,128)} %bitcast.51), kind=kOutput, calls=%fused_computation.12 | convolution fusion | flops 805308416 | bytes 16777600 | tf_op jit(solution)/shard_map/dot_general | solution.py:17
  428.0 10.8 copy.36
  438.8 10.7 copy.54
  449.5 11.9 %sub.79 = f32[2048,1024]{0,1:T(8,128)} subtract(f32[2048,1024]{0,1:T(8,128)} %copy.37, f32[2048,1024]{0,1:T(8,128)} %bitcast.170) | non-fusion elementwise | flops 2097152 | bytes 25165824 | tf_op jit(solution)/shard_map/sub | solution.py:100
  463.5 11.7 %cholesky.130 = f32[128,128]{1,0:T(8,128)S(1)} custom-call(f32[128,128]{1,0:T(8,128)S(1)} %cholesky.194), custom_call_target="Cholesky" | custom-call | tf_op jit(solution)/shard_map/jit(cholesky)/cholesky | solution.py:110
  475.2 10.0 custom-call.13
  485.7 11.7 %cholesky.147 = f32[128,128]{1,0:T(8,128)S(1)} custom-call(f32[128,128]{1,0:T(8,128)S(1)} %convolution_subtract_fusion.5), custom_call_target="Cholesky" | custom-call | tf_op jit(solution)/shard_map/jit(cholesky)/cholesky | solution.py:110
  503.6 19.7 %custom-call.14 = f32[2,128,128]{1,2,0:T(8,128)S(1)} custom-call(f32[2,128,128]{2,1,0:T(8,128)S(1)} %get-tuple-element.42), custom_call_target="InvertDiagBlocksLowerTriangular" | custom-call | tf_op jit(solution)/shard_map/triangular_solve/custom-call.0 | solution.py:111
  525.3 63.0 %all-reduce.8.cloned.1.call-done = f32[2,256,256]{2,1,0:T(8,128)} async-done(((f32[2,256,256]{2,1,0:T(8,128)}), f32[2,256,256]{2,1,0:T(8,128)}) %all-reduce.8.cloned.1.call-update) | async-done | bytes 524304 | tf_op jit(solution)/shard_map/psum | solution.py:13
  595.1 89.7 %all-reduce.10.cloned.1.call-done = f32[2048,256]{1,0:T(8,128)} async-done(((f32[2048,256]{1,0:T(8,128)}), f32[2048,256]{1,0:T(8,128)}) %all-reduce.10.cloned.1.call-update) | async-done | bytes 2097168 | tf_op jit(solution)/shard_map/psum | solution.py:13
  688.1 64.6 %all-reduce.12.cloned.1.call-done = f32[2048,256]{1,0:T(8,128)} async-done(((f32[2048,256]{1,0:T(8,128)}), f32[2048,256]{1,0:T(8,128)}) %all-reduce.12.cloned.1.call-update) | async-done | bytes 2097168 | tf_op jit(solution)/shard_map/psum | solution.py:13
  752.7 10.5 convolution_subtract_fusion.1
  767.7 11.7 %cholesky.164 = f32[128,128]{1,0:T(8,128)S(1)} custom-call(f32[128,128]{1,0:T(8,128)S(1)} %cholesky.197), custom_call_target="Cholesky" | custom-call | tf_op jit(solution)/shard_map/jit(cholesky)/cholesky | solution.py:110
  780.1 9.8 custom-call.15
  790.4 11.7 %cholesky.181 = f32[128,128]{1,0:T(8,128)S(1)} custom-call(f32[128,128]{1,0:T(8,128)S(1)} %convolution_subtract_fusion.4), custom_call_target="Cholesky" | custom-call | tf_op jit(solution)/shard_map/jit(cholesky)/cholesky | solution.py:110
  808.4 19.9 %custom-call.16 = f32[2,128,128]{1,2,0:T(8,128)S(1)} custom-call(f32[2,128,128]{2,1,0:T(8,128)S(1)} %get-tuple-element.43), custom_call_target="InvertDiagBlocksLowerTriangular" | custom-call | tf_op jit(solution)/shard_map/triangular_solve/custom-call.0 | solution.py:111
  830.3 60.3 %all-reduce.14.cloned.1.call-done = f32[2,256,256]{2,1,0:T(8,128)} async-done(((f32[2,256,256]{2,1,0:T(8,128)}), f32[2,256,256]{2,1,0:T(8,128)}) %all-reduce.14.cloned.1.call-update) | async-done | bytes 524304 | tf_op jit(solution)/shard_map/psum | solution.py:13
  897.3 89.8 %all-reduce.16.cloned.1.call-done = f32[2048,256]{1,0:T(8,128)} async-done(((f32[2048,256]{1,0:T(8,128)}), f32[2048,256]{1,0:T(8,128)}) %all-reduce.16.cloned.1.call-update) | async-done | bytes 2097168 | tf_op jit(solution)/shard_map/psum | solution.py:13
  994.4 59.9 %all-reduce.18.cloned.1.call-done = f32[2048,256]{1,0:T(8,128)} async-done(((f32[2048,256]{1,0:T(8,128)}), f32[2048,256]{1,0:T(8,128)}) %all-reduce.18.cloned.1.call-update) | async-done | bytes 2097168 | tf_op jit(solution)/shard_map/psum | solution.py:13
  1054.2 11.8 %convolution_subtract_fusion = f32[2048,1024]{0,1:T(8,128)} fusion(f32[2048,1024]{0,1:T(8,128)} %copy-done.2, f32[2048,256]{1,0:T(8,128)} %all-reduce.16.cloned.1.call-done, f32[2048,256]{1,0:T(8,128)} %all-reduce.18.cloned.1.call-done, s32[]{:T(128)S(6)} %select_n.189), kind=kOutput, calls=%fused_computation.9 | convolution fusion | flops 6444548096 | bytes 19922948 | tf_op jit(solution)/shard_map/dot_general | solution.py:23
  (124 shorter events, 125.3 us)
Async XLA Ops:
  7.2 1.2 copy-start
  15.0 8.3 copy-start.6
  15.0 156.0 %all-to-all-start = ((f32[16,256,512]{2,1,0:T(8,128)}), f32[16,256,512]{2,1,0:T(8,128)}, u32[]{:S(2)}, u32[]{:S(2)}) async-start(f32[16,256,512]{2,1,0:T(8,128)} %stack.14), calls=%async_computation | async-start | bytes 16777216 | tf_op jit(solution)/shard_map/all_to_all | solution.py:54
  186.5 54.4 %all-to-all-start.1 = ((f32[8,2,256,256]{3,2,1,0:T(8,128)}), f32[8,2,256,256]{3,2,1,0:T(8,128)}, u32[]{:S(2)}, u32[]{:S(2)}) async-start(f32[8,2,256,256]{3,2,1,0:T(8,128)} %bitcast.172), calls=%async_computation.1 | async-start | bytes 8388608 | tf_op jit(solution)/shard_map/all_to_all | solution.py:67
  257.3 153.4 %all-to-all-start.2 = ((f32[16,2,256,256]{3,2,1,0:T(8,128)}), f32[16,2,256,256]{3,2,1,0:T(8,128)}, u32[]{:S(2)}, u32[]{:S(2)}) async-start(f32[16,2,256,256]{3,2,1,0:T(8,128)} %copy.34), calls=%async_computation.2 | async-start | bytes 16777216 | tf_op jit(solution)/shard_map/all_to_all | solution.py:80
  265.6 322.7 %all-reduce.8.cloned.1.call-start = ((), (), s32[]{:S(2)}) async-start(), calls=%async_computation.3 | async-start | bytes 1048576 | tf_op jit(solution)/shard_map/psum | solution.py:13
  525.2 159.6 %all-reduce.10.cloned.1.call-start = ((), (), s32[]{:S(2)}) async-start(), calls=%async_computation.4 | async-start | bytes 4194304 | tf_op jit(solution)/shard_map/psum | solution.py:13
  588.3 5.2 copy-start.5
  595.0 157.7 %all-reduce.12.cloned.1.call-start = ((), (), s32[]{:S(2)}) async-start(), calls=%async_computation.5 | async-start | bytes 4194304 | tf_op jit(solution)/shard_map/psum | solution.py:13
  684.8 67.9 %copy-start.3 = (f32[2048,256]{1,0:T(8,128)S(1)}, f32[2048,256]{1,0:T(8,128)}, u32[]{:S(2)}) copy-start(f32[2048,256]{1,0:T(8,128)} %all-reduce.10.cloned.1.call-done) | copy-start | bytes 6291460
  688.0 202.6 %all-reduce.14.cloned.1.call-start = ((), (), s32[]{:S(2)}) async-start(), calls=%async_computation.6 | async-start | bytes 1048576 | tf_op jit(solution)/shard_map/psum | solution.py:13
  763.1 3.4 copy-start.2
  830.3 156.8 %all-reduce.16.cloned.1.call-start = ((), (), s32[]{:S(2)}) async-start(), calls=%async_computation.7 | async-start | bytes 4194304 | tf_op jit(solution)/shard_map/psum | solution.py:13
  890.6 5.2 copy-start.4
  897.3 156.9 %all-reduce.18.cloned.1.call-start = ((), (), s32[]{:S(2)}) async-start(), calls=%async_computation.8 | async-start | bytes 4194304 | tf_op jit(solution)/shard_map/psum | solution.py:13
  1066.0 9.3 copy-start.1
Sparse Core Ops, SparseCore 0:
  525.3 62.9 all-reduce.7
  595.1 89.6 all-reduce.9
  688.1 64.4 all-reduce.11
  830.4 60.1 all-reduce.13
  897.4 89.6 all-reduce.15
  990.3 63.8 all-reduce.17
